TPU v7x, 32 devices: a whole 2x2x4 slice. The times are simulated.
32 devices in a mesh: dp: 8 (over z, x), ctx: 4 (over y, core).
Axes of the slice: x: 2, y: 2, z: 4, core: 2. Of those that a mesh axis runs over, the one named last changes fastest.
Arguments:
- inputs: bfloat16 [8, 512, 5376], P('dp', 'ctx'), may hold values from -6 to 6
- q_proj: bfloat16 [8, 512, 2048], P('dp', 'ctx'), may hold values from -260 to 260
- k_proj: bfloat16 [8, 512, 1024], P('dp', 'ctx'), may hold values from -260 to 260
- v_proj: bfloat16 [8, 512, 1024], P('dp', 'ctx'), may hold values from -6 to 6
- d_attn: bfloat16 [8, 512, 2048], P('dp', 'ctx'), may hold values from -6 to 6
- positions: int32 [8, 512], P('dp', 'ctx'), may hold values from 0 to 511, as said below
- windows: int32 [8], P('dp'), may hold values from 512 to 1024
- q_gain: float32 [128], replicated, may hold values from 0.7 to 5.5
- k_gain: float32 [128], replicated, may hold values from 0.7 to 5.5
- weight: bfloat16 [5376, 4096], P('dp'), may hold values from -0.078125 to 0.078125
Outputs:
- d_inputs: bfloat16 [8, 512, 5376], P('dp', 'ctx')
- d_weight_t: float32 [4096, 5376], P('ctx', 'dp')
- d_q_gain: float32 [128], replicated
- d_k_gain: float32 [128], replicated
Inputs may be any that keep to these rules, and one draw needn't show every extreme that they name: `positions`: within each sequence a position counts the tokens since its document began: it grows by one from token to token and falls to 0 where a document begins; the first token of a sequence has position 0. Some sequence holds a single document.
All inputs are finite; a program needn't handle non-finite values.
Results may differ from a plain program's by a relative error of at most 0.029.
Values may be sent and summed in bfloat16 or wider, within the bound.
A program may use at most 128 MiB of HBM per device.

v0:
```python
import math
import jax
import jax.numpy as jnp
from jax import lax
from jax.sharding import PartitionSpec as P

REACH = 8
score_scale = 168.0 ** (-0.5)
rope_base = 10000.0
norm_eps = 1e-06


def from_behind(value, axis, steps):
    count = lax.axis_size(axis)
    initial, last = (max(0, -steps), min(count, count - steps))
    return lax.ppermute(value, axis, [(source, source + steps) for source in range(initial, last)])


def rotated_unit(projected_rows, gain_vector, token_pos, head_count):
    head_width = gain_vector.shape[0]
    rows_heads = projected_rows.reshape(projected_rows.shape[0], head_count, head_width)
    inverse = lax.rsqrt(jnp.mean(rows_heads * rows_heads, axis=-1, keepdims=True) + norm_eps)
    normed = rows_heads * inverse * gain_vector
    half_width = head_width // 2
    frequency = jnp.exp(
        jnp.arange(half_width, dtype=jnp.float32) * (-2.0 * math.log(rope_base) / head_width)
    )
    angles = token_pos.astype(jnp.float32)[:, None] * frequency[None, :]
    cosine_table = jnp.cos(angles)[:, None, :]
    sine_table = jnp.sin(angles)[:, None, :]
    first_half = normed[..., :half_width]
    second_half = normed[..., half_width:]
    return jnp.concatenate(
        [
            first_half * cosine_table - second_half * sine_table,
            second_half * cosine_table + first_half * sine_table,
        ],
        axis=-1,
    )


def shards(inputs, q_proj, k_proj, v_proj, d_attn, positions, windows, q_gain, k_gain, weight):
    tok_rows = inputs.shape[1]
    head_width = q_gain.shape[0]
    query_heads = q_proj.shape[2] // head_width
    key_heads = k_proj.shape[2] // head_width
    group_size = query_heads // key_heads
    token_pos = positions[0]
    window = windows[0]
    input_cols = lax.all_to_all(inputs, "dp", split_axis=2, concat_axis=0, tiled=True)

    def query_side(projected_rows, gain_vector):
        return rotated_unit(projected_rows, gain_vector, token_pos, query_heads)

    def key_side(projected_rows, gain_vector):
        return rotated_unit(projected_rows, gain_vector, token_pos, key_heads)

    q_full, query_back = jax.vjp(query_side, q_proj[0].astype(jnp.float32), q_gain)
    k_full, key_back = jax.vjp(key_side, k_proj[0].astype(jnp.float32), k_gain)
    query_rotated = q_full.astype(jnp.bfloat16).reshape(tok_rows, key_heads, group_size, head_width)
    key_rotated = k_full.astype(jnp.bfloat16)
    v_own = v_proj[0].reshape(tok_rows, key_heads, head_width)
    reach_count = min(REACH, lax.axis_size("ctx") - 1)
    key_blocks = [key_rotated]
    value_blocks = [v_own]
    for distance_steps in range(1, reach_count + 1):
        far_keys, far_values = from_behind((key_rotated, v_own), "ctx", distance_steps)
        key_blocks.append(far_keys)
        value_blocks.append(far_values)
    all_keys = jnp.stack(key_blocks)
    all_values = jnp.stack(value_blocks)
    block_ids = jnp.arange(reach_count + 1, dtype=jnp.int32)
    offsets = jnp.arange(tok_rows, dtype=jnp.int32)
    distance = block_ids[None, :, None] * tok_rows + offsets[:, None, None] - offsets[None, None, :]
    allowed = (distance >= 0) & (distance < window) & (distance <= token_pos[:, None, None])
    scores = (
        jnp.einsum("ahgd,bchd->hgabc", query_rotated, all_keys, preferred_element_type=jnp.float32)
        * score_scale
    )
    scores = jnp.where(allowed, scores, -jnp.inf)
    row_max = jnp.max(scores, axis=(3, 4), keepdims=True)
    exponent = jnp.exp(scores - row_max)
    probs = exponent / jnp.sum(exponent, axis=(3, 4), keepdims=True)
    head_gradient = d_attn[0].reshape(tok_rows, key_heads, group_size, head_width)
    dprobs = jnp.einsum(
        "ahgd,bchd->hgabc", head_gradient, all_values, preferred_element_type=jnp.float32
    )
    delta = jnp.sum(probs * dprobs, axis=(3, 4), keepdims=True)
    dscores = (probs * (dprobs - delta)).astype(jnp.bfloat16)
    probs_low = probs.astype(jnp.bfloat16)
    dq_rot = (
        jnp.einsum("hgabc,bchd->ahgd", dscores, all_keys, preferred_element_type=jnp.float32)
        * score_scale
    )
    dk_blocks = (
        jnp.einsum("hgabc,ahgd->bchd", dscores, query_rotated, preferred_element_type=jnp.float32)
        * score_scale
    )
    dv_blocks = jnp.einsum(
        "hgabc,ahgd->bchd", probs_low, head_gradient, preferred_element_type=jnp.float32
    )
    dk_total = dk_blocks[0]
    dv_total = dv_blocks[0]
    for distance_steps in range(1, reach_count + 1):
        back_keys, back_values = from_behind(
            (
                dk_blocks[distance_steps].astype(jnp.bfloat16),
                dv_blocks[distance_steps].astype(jnp.bfloat16),
            ),
            "ctx",
            -distance_steps,
        )
        dk_total = dk_total + back_keys.astype(jnp.float32)
        dv_total = dv_total + back_values.astype(jnp.float32)
    dq_proj, dq_gain = query_back(dq_rot.reshape(tok_rows, query_heads, head_width))
    dk_proj, dk_gain = key_back(dk_total)
    dq_gain_all, dk_gain_all = lax.psum((dq_gain, dk_gain), ("dp", "ctx"))
    dv_proj = dv_total.reshape(tok_rows, key_heads * head_width)
    d_proj = jnp.concatenate([dq_proj, dk_proj, dv_proj], axis=-1).astype(jnp.bfloat16)[None]
    gathered = lax.all_gather(d_proj, "dp", axis=0, tiled=True)
    d_cols = jnp.einsum("btp,dp->btd", gathered, weight, preferred_element_type=jnp.float32)
    d_inputs = lax.all_to_all(
        d_cols.astype(jnp.bfloat16), "dp", split_axis=0, concat_axis=2, tiled=True
    )
    d_weight_t = lax.psum_scatter(
        jnp.einsum("btp,btd->pd", gathered, input_cols, preferred_element_type=jnp.float32).astype(
            jnp.bfloat16
        ),
        "ctx",
        scatter_dimension=0,
        tiled=True,
    ).astype(jnp.float32)
    return (d_inputs, d_weight_t, dq_gain_all, dk_gain_all)


def solution(mesh):
    placed = (
        P("dp", "ctx", None),
        P("dp", "ctx", None),
        P("dp", "ctx", None),
        P("dp", "ctx", None),
        P("dp", "ctx", None),
        P("dp", "ctx"),
        P("dp"),
        P(),
        P(),
        P("dp", None),
    )
    return jax.shard_map(
        shards,
        mesh=mesh,
        in_specs=placed,
        out_specs=(P("dp", "ctx", None), P("ctx", "dp"), P(), P()),
        check_vma=False,
    )
```

profile of v0, /device:TPU:0, one launch (start us, length us, event | category | flops | bytes accessed | tf_op | source)
XLA Modules:
  0.0 321.0 jit_solution(8718791477971543858)
XLA Ops:
  7.2 1.2 copy.176
  11.7 5.0 %collective-permute-start.2 = (bf16[128,8,128]{2,0,1:T(8,128)(2,1)}, bf16[128,8,128]{2,0,1:T(8,128)(2,1)}, u32[]{:S(2)}, u32[]{:S(2)}) collective-permute-start(bf16[128,8,128]{2,0,1:T(8,128)(2,1)} %pad_maximum_fusion.3), channel_id=1, source_target_pairs={{0,3},{4,7},{8,11},{12,15},{16,19},{20,23},{24,27},{28,31}} | collective-permute-start | bytes 786440 | tf_op jit(solution)/shard_map/ppermute | solution.py:16
  16.7 2.0 collective-permute-start
  18.7 2.0 collective-permute-start.1
  21.7 2.0 collective-permute-start.3
  23.6 2.0 collective-permute-start.4
  28.5 1.4 reshape_squeeze.7
  29.9 1.2 copy.224
  31.4 1.5 collective-permute-start.5
  32.9 2.1 fusion.7
  35.9 3.9 %collective-permute-done.5 = bf16[128,8,128]{2,0,1:T(8,128)(2,1)S(1)} collective-permute-done((bf16[128,8,128]{2,0,1:T(8,128)(2,1)}, bf16[128,8,128]{2,0,1:T(8,128)(2,1)S(1)}, u32[]{:S(2)}, u32[]{:S(2)}) %collective-permute-start.5) | collective-permute-done | bytes 262176 | tf_op jit(solution)/shard_map/ppermute | solution.py:16
  39.8 2.4 fusion.2
  42.2 1.3 fusion.4
  43.6 1.7 fusion.21
  45.2 2.2 fusion.57
  47.4 3.0 fusion.56
  50.5 1.4 copy.237
  51.9 1.4 copy.238
  53.3 0.9 slice_bitcast_fusion.7
  54.2 1.3 collective-permute-start.6
  55.5 1.3 collective-permute-start.7
  56.8 1.3 collective-permute-start.8
  58.1 1.8 multiply_add_fusion.1
  60.9 1.8 fusion.22
  62.7 1.3 concatenate.51
  64.0 1.2 slice_bitcast_fusion.4
  65.2 1.3 collective-permute-start.10
  66.5 1.3 collective-permute-start.11
  67.8 1.3 collective-permute-start.9
  69.3 1.7 collective-permute-done.8
  71.0 1.4 fusion.40
  74.0 2.3 collective-permute-done.10
  76.3 6.4 %collective-permute-done.11 = bf16[128,8,128]{0,2,1:T(8,128)(2,1)S(1)} collective-permute-done((bf16[128,8,128]{0,2,1:T(8,128)(2,1)S(1)}, bf16[128,8,128]{0,2,1:T(8,128)(2,1)S(1)}, u32[]{:S(2)}, u32[]{:S(2)}) %collective-permute-start.11) | collective-permute-done | bytes 262176 | tf_op jit(solution)/shard_map/ppermute | solution.py:16
  82.7 1.2 fusion.37
  84.0 1.0 pad_maximum_fusion.1
  85.4 6.3 %copy.211 = bf16[1,128,5376]{1,0,2:T(2,128)(2,1)S(1)} copy(bf16[1,128,5376]{2,1,0:T(8,128)(2,1)} %param.10) | data formatting | bytes 2752512 | tf_op args[0]
  92.2 30.3 %reduce = bf16[5376,128]{1,0:T(8,128)(2,1)} reduce(bf16[5376,1,128]{2,1,0:T(2,128)(2,1)S(1)} %bitcast.178, bf16[]{:T(256)} %broadcast.142), dimensions={1}, to_apply=%bitcast.157.reduce_sub_computation | reduce | bytes 2752514
  122.4 3.2 %reshape.256 = bf16[8,2,43008]{2,1,0:T(2,128)(2,1)S(1)} reshape(bf16[5376,128]{1,0:T(8,128)(2,1)} %reduce) | data formatting | bytes 2752512
  125.7 71.0 %all_to_all.36 = bf16[8,2,43008]{2,1,0:T(2,128)(2,1)} all-to-all(bf16[8,2,43008]{2,1,0:T(2,128)(2,1)S(1)} %reshape.256), channel_id=1, replica_groups=mesh['dp'=8,'ctx'=4] {'dp'}, dimensions={0} | all-to-all | bytes 2752512 | tf_op jit(solution)/shard_map/all_to_all | solution.py:50
  196.7 4.5 %reshape.257 = bf16[5376,1,128]{2,1,0:T(2,128)(2,1)S(1)} reshape(bf16[8,2,43008]{2,1,0:T(2,128)(2,1)} %all_to_all.36) | data formatting | bytes 2752512
  201.2 1.3 copy.236
  202.5 29.1 %all-gather.2.cloned.1.call-done = bf16[8,128,4096]{2,1,0:T(8,128)(2,1)} async-done(((bf16[1,128,4096]{2,1,0:T(8,128)(2,1)}), bf16[8,128,4096]{2,1,0:T(8,128)(2,1)}) %all-gather.2.cloned.1.call-update) | async-done | bytes 8388624 | tf_op jit(solution)/shard_map/all_gather | solution.py:120
  231.6 10.2 %bitcast_convert_fusion = bf16[4096,672]{0,1:T(8,128)(2,1)} fusion(bf16[8,128,672]{1,2,0:T(8,128)(2,1)} %bitcast.192, bf16[8,128,4096]{2,1,0:T(8,128)(2,1)} %all-gather.2.cloned.1.call-done), kind=kOutput, calls=%fused_computation | convolution fusion | flops 5639897088 | bytes 15269888 | tf_op jit(solution)/shard_map/btp,btd->pd/dot_general | solution.py:126
  241.8 11.1 %fusion.18 = bf16[8,128,672]{1,2,0:T(8,128)(2,1)} fusion(bf16[8,128,4096]{2,1,0:T(8,128)(2,1)} %all-gather.2.cloned.1.call-done, bf16[672,4096]{1,0:T(8,128)(2,1)} %param.19), kind=kOutput, calls=%fused_computation.20 | convolution fusion | flops 5637832704 | bytes 15269888 | tf_op jit(solution)/shard_map/btp,dp->btd/dot_general | solution.py:121
  252.9 3.6 %all-to-all-start = ((bf16[8,128,672]{1,2,0:T(8,128)(2,1)}), bf16[8,128,672]{1,2,0:T(8,128)(2,1)S(1)}, u32[]{:S(2)}, u32[]{:S(2)}) async-start(bf16[8,128,672]{1,2,0:T(8,128)(2,1)} %fusion.18), calls=%async_computation | async-start | bytes 2752512 | tf_op jit(solution)/shard_map/all_to_all | solution.py:122
  256.4 53.0 %all-reduce.4 = (f32[128]{0:T(128)}, f32[128]{0:T(128)}) all-reduce(f32[128]{0:T(128)S(1)} %get-tuple-element.28, f32[128]{0:T(128)S(1)} %get-tuple-element.30), channel_id=1, replica_groups=mesh['dp'=8,'ctx'=4] {'dp','ctx'}, use_global_device_ids=true, to_apply=%region_9.10 | all-reduce | flops 256 | bytes 2048 | tf_op jit(solution)/shard_map/psum | solution.py:117
  309.5 1.5 copy.212
  311.0 3.2 %convert_element_type.126 = f32[1024,672]{0,1:T(8,128)} convert(bf16[1024,672]{0,1:T(8,128)(2,1)} %reduce-scatter.2.cloned.1.call-done) | non-fusion elementwise | flops 688128 | bytes 4128768 | tf_op jit(solution)/shard_map/convert_element_type | solution.py:132
  (70 shorter events, 11.5 us)
Async XLA Ops:
  7.2 13.5 %copy-start.4 = (bf16[1,128,1024]{2,1,0:T(8,128)(2,1)S(1)}, bf16[1,128,1024]{2,1,0:T(8,128)(2,1)}, u32[]{:S(2)}) copy-start(bf16[1,128,1024]{2,1,0:T(8,128)(2,1)} %param.13) | copy-start | bytes 786436
  7.2 18.5 %copy-start.2 = (bf16[1,128,2048]{2,1,0:T(8,128)(2,1)S(1)}, bf16[1,128,2048]{2,1,0:T(8,128)(2,1)}, u32[]{:S(2)}) copy-start(bf16[1,128,2048]{2,1,0:T(8,128)(2,1)} %param.11) | copy-start | bytes 1572868
  7.2 224.4 %all-gather.2.cloned.1.call-start = ((), (), s32[]{:S(2)}) async-start(), calls=%async_computation.3 | async-start | bytes 9437184 | tf_op jit(solution)/shard_map/all_gather | solution.py:120
  8.6 17.0 %copy-start = (f32[128,8,128]{2,0,1:T(8,128)}, f32[128,8,128]{2,0,1:T(8,128)S(1)}, u32[]{:S(2)}) copy-start(f32[128,8,128]{2,0,1:T(8,128)S(1)} %copy.177) | copy-start | bytes 1572868
  10.5 15.9 %copy-start.5 = (f32[128]{0:T(128)S(1)}, f32[128]{0:T(128)}, u32[]{:S(2)}) copy-start(f32[128]{0:T(128)} %param.17) | copy-start | bytes 1540
  11.7 19.7 %collective-permute-start.2 = (bf16[128,8,128]{2,0,1:T(8,128)(2,1)}, bf16[128,8,128]{2,0,1:T(8,128)(2,1)}, u32[]{:S(2)}, u32[]{:S(2)}) collective-permute-start(bf16[128,8,128]{2,0,1:T(8,128)(2,1)} %pad_maximum_fusion.3), channel_id=1, source_target_pairs={{0,3},{4,7},{8,11},{12,15},{16,19},{20,23},{24,27},{28,31}} | collective-permute-start | bytes 786440 | tf_op jit(solution)/shard_map/ppermute | solution.py:16
  16.7 16.2 %collective-permute-start = (bf16[128,8,128]{2,0,1:T(8,128)(2,1)}, bf16[128,8,128]{2,0,1:T(8,128)(2,1)}, u32[]{:S(2)}, u32[]{:S(2)}) collective-permute-start(bf16[128,8,128]{2,0,1:T(8,128)(2,1)} %pad_maximum_fusion.3), channel_id=1, source_target_pairs={{0,1},{1,2},{2,3},{4,5},{5,6},{6,7},{8,9},{9,10},{10,11},{12,13},{... | collective-permute-start | bytes 786440 | tf_op jit(solution)/shard_map/ppermute | solution.py:16
  18.7 14.3 %collective-permute-start.1 = (bf16[128,8,128]{2,0,1:T(8,128)(2,1)}, bf16[128,8,128]{2,0,1:T(8,128)(2,1)}, u32[]{:S(2)}, u32[]{:S(2)}) collective-permute-start(bf16[128,8,128]{2,0,1:T(8,128)(2,1)} %pad_maximum_fusion.3), channel_id=1, source_target_pairs={{0,2},{1,3},{4,6},{5,7},{8,10},{9,11},{12,14},{13,15},{16,18},{17,... | collective-permute-start | bytes 786440 | tf_op jit(solution)/shard_map/ppermute | solution.py:16
  21.7 14.2 %collective-permute-start.3 = (bf16[128,8,128]{2,0,1:T(8,128)(2,1)}, bf16[128,8,128]{2,0,1:T(8,128)(2,1)}, u32[]{:S(2)}, u32[]{:S(2)}) collective-permute-start(bf16[128,8,128]{2,0,1:T(8,128)(2,1)} %copy.187), channel_id=1, source_target_pairs={{0,1},{1,2},{2,3},{4,5},{5,6},{6,7},{8,9},{9,10},{10,11},{12,13},{... | collective-permute-start | bytes 786440 | tf_op jit(solution)/shard_map/ppermute | solution.py:16
  23.6 12.3 %collective-permute-start.4 = (bf16[128,8,128]{2,0,1:T(8,128)(2,1)}, bf16[128,8,128]{2,0,1:T(8,128)(2,1)}, u32[]{:S(2)}, u32[]{:S(2)}) collective-permute-start(bf16[128,8,128]{2,0,1:T(8,128)(2,1)} %copy.187), channel_id=1, source_target_pairs={{0,2},{1,3},{4,6},{5,7},{8,10},{9,11},{12,14},{13,15},{16,18},{17,... | collective-permute-start | bytes 786440 | tf_op jit(solution)/shard_map/ppermute | solution.py:16
  26.8 4.5 %copy-start.7 = (s32[1,128]{1,0:T(1,128)S(1)}, s32[1,128]{1,0:T(1,128)}, u32[]{:S(2)}) copy-start(s32[1,128]{1,0:T(1,128)} %param.15) | copy-start | bytes 1540
  31.4 8.4 %collective-permute-start.5 = (bf16[128,8,128]{2,0,1:T(8,128)(2,1)}, bf16[128,8,128]{2,0,1:T(8,128)(2,1)S(1)}, u32[]{:S(2)}, u32[]{:S(2)}) collective-permute-start(bf16[128,8,128]{2,0,1:T(8,128)(2,1)} %copy.187), channel_id=1, source_target_pairs={{0,3},{4,7},{8,11},{12,15},{16,19},{20,23},{24,27},{28,31}} | collective-permute-start | bytes 786440 | tf_op jit(solution)/shard_map/ppermute | solution.py:16
  35.0 4.8 %copy-start.3 = (bf16[128,8,2,128,1]{0,3,2,4,1:T(8,128)(2,1)S(1)}, bf16[128,8,2,128,1]{0,3,2,4,1:T(8,128)(2,1)}, u32[]{:S(2)}) copy-start(bf16[128,8,2,128,1]{0,3,2,4,1:T(8,128)(2,1)} %copy.224) | copy-start | bytes 1572868
  54.2 13.7 %collective-permute-start.6 = (bf16[128,8,128]{2,0,1:T(8,128)(2,1)}, bf16[128,8,128]{2,0,1:T(8,128)(2,1)}, u32[]{:S(2)}, u32[]{:S(2)}) collective-permute-start(bf16[128,8,128]{2,0,1:T(8,128)(2,1)} %get-tuple-element.40), channel_id=1, source_target_pairs={{1,0},{2,1},{3,2},{5,4},{6,5},{7,6},{9,8},{10,9},{11,10},{13,12},{... | collective-permute-start | bytes 786440 | tf_op jit(solution)/shard_map/ppermute | solution.py:16
  55.5 13.8 %collective-permute-start.7 = (bf16[128,8,128]{2,0,1:T(8,128)(2,1)}, bf16[128,8,128]{2,0,1:T(8,128)(2,1)}, u32[]{:S(2)}, u32[]{:S(2)}) collective-permute-start(bf16[128,8,128]{2,0,1:T(8,128)(2,1)} %get-tuple-element.42), channel_id=1, source_target_pairs={{2,0},{3,1},{6,4},{7,5},{10,8},{11,9},{14,12},{15,13},{18,16},{19,... | collective-permute-start | bytes 786440 | tf_op jit(solution)/shard_map/ppermute | solution.py:16
  56.8 14.2 %collective-permute-start.8 = (bf16[128,8,128]{2,0,1:T(8,128)(2,1)}, bf16[128,8,128]{2,0,1:T(8,128)(2,1)}, u32[]{:S(2)}, u32[]{:S(2)}) collective-permute-start(bf16[128,8,128]{2,0,1:T(8,128)(2,1)} %get-tuple-element.41), channel_id=1, source_target_pairs={{3,0},{7,4},{11,8},{15,12},{19,16},{23,20},{27,24},{31,28}} | collective-permute-start | bytes 786440 | tf_op jit(solution)/shard_map/ppermute | solution.py:16
  62.7 9.9 %copy-start.1 = (f32[128,8,128]{2,0,1:T(8,128)S(1)}, f32[128,8,128]{2,0,1:T(8,128)}, u32[]{:S(2)}) copy-start(f32[128,8,128]{2,0,1:T(8,128)} %copy-done) | copy-start | bytes 1572868
  62.7 9.9 %copy-start.6 = (f32[128]{0:T(128)S(1)}, f32[128]{0:T(128)}, u32[]{:S(2)}) copy-start(f32[128]{0:T(128)} %param.18) | copy-start | bytes 1540
  65.2 11.1 %collective-permute-start.10 = (bf16[128,8,128]{0,2,1:T(8,128)(2,1)S(1)}, bf16[128,8,128]{0,2,1:T(8,128)(2,1)S(1)}, u32[]{:S(2)}, u32[]{:S(2)}) collective-permute-start(bf16[128,8,128]{0,2,1:T(8,128)(2,1)S(1)} %get-tuple-element.45), channel_id=1, source_target_pairs={{2,0},{3,1},{6,4},{7,5},{10,8},{11,9},{14,12},{15,13},{18,16},{19,... | collective-permute-start | bytes 786440 | tf_op jit(solution)/shard_map/ppermute | solution.py:16
  66.5 16.2 %collective-permute-start.11 = (bf16[128,8,128]{0,2,1:T(8,128)(2,1)S(1)}, bf16[128,8,128]{0,2,1:T(8,128)(2,1)S(1)}, u32[]{:S(2)}, u32[]{:S(2)}) collective-permute-start(bf16[128,8,128]{0,2,1:T(8,128)(2,1)S(1)} %get-tuple-element.44), channel_id=1, source_target_pairs={{3,0},{7,4},{11,8},{15,12},{19,16},{23,20},{27,24},{31,28}} | collective-permute-start | bytes 786440 | tf_op jit(solution)/shard_map/ppermute | solution.py:16
  67.8 14.9 %collective-permute-start.9 = (bf16[128,8,128]{0,2,1:T(8,128)(2,1)S(1)}, bf16[128,8,128]{0,2,1:T(8,128)(2,1)S(1)}, u32[]{:S(2)}, u32[]{:S(2)}) collective-permute-start(bf16[128,8,128]{0,2,1:T(8,128)(2,1)S(1)} %get-tuple-element.43), channel_id=1, source_target_pairs={{1,0},{2,1},{3,2},{5,4},{6,5},{7,6},{9,8},{10,9},{11,10},{13,12},{... | collective-permute-start | bytes 786440 | tf_op jit(solution)/shard_map/ppermute | solution.py:16
  85.1 225.9 %reduce-scatter.2.cloned.1.call-start = ((), (), s32[]{:S(2)}) async-start(), calls=%async_computation.4 | async-start | bytes 6881280 | tf_op jit(solution)/shard_map/reduce_scatter | solution.py:125
  252.9 56.6 %all-to-all-start = ((bf16[8,128,672]{1,2,0:T(8,128)(2,1)}), bf16[8,128,672]{1,2,0:T(8,128)(2,1)S(1)}, u32[]{:S(2)}, u32[]{:S(2)}) async-start(bf16[8,128,672]{1,2,0:T(8,128)(2,1)} %fusion.18), calls=%async_computation | async-start | bytes 2752512 | tf_op jit(solution)/shard_map/all_to_all | solution.py:122
Sparse Core Ops, SparseCore 0:
  85.2 146.3 all-gather.1
  241.9 51.8 reduce-scatter.1
where the time goes:
time: 322 us; the launch traced here: 321 us
  blocking collectives  124 us (39%)
  other arithmetic  49.7 us (15%)
  waiting for transfers between devices  43.6 us (14%)
  matrix products  32.5 us (10%)
  local copies, waits for them, and re-layouts  30 us (9%)
  starting transfers between devices  26 us (8%)
  between operations  15.2 us (5%)
    all_to_all x1, blocking collectives, shards(): lax.all_to_all(inputs, 'dp', split_axis=2, concat_axis=0, tiled=True)  71 us
    psum x1, blocking collectives, shards(): dq_gain_all, dk_gain_all = lax.psum((dq_gain, dk_gain), ('dp', 'ctx'))  53 us
    unnamed x2, other arithmetic  30.4 us
    all_gather x1, waiting for transfers between devices, shards(): gathered = lax.all_gather(d_proj, 'dp', axis=0, tiled=True)  29.1 us
    ppermute x12, starting transfers between devices, from_behind(): lax.ppermute(value, axis, [(source, source + steps) for source in range(i...  22.2 us
    unnamed x27, local copies, waits for them, and re-layouts  21.7 us
    ppermute x12, waiting for transfers between devices, from_behind(): lax.ppermute(value, axis, [(source, source + steps) for source in range(i...  14.4 us
    dot_general x1, matrix products, shards(): jnp.einsum('btp,dp->btd', gathered, weight, preferred_element_type=jnp.fl...  11.1 us
  transfers between devices with their start and end apart: 15, of which 6 were waited for; matrix products, arithmetic and copies ran while one was open for 24% of the time, Pallas kernels for 0%

commit v1 on v0

--- a/solution.py
+++ b/solution.py
@@ -47,7 +47,10 @@
     group_size = query_heads // key_heads
     token_pos = positions[0]
     window = windows[0]
-    input_cols = lax.all_to_all(inputs, "dp", split_axis=2, concat_axis=0, tiled=True)
+    input_cols = jnp.concatenate(
+        lax.all_to_all(jnp.stack(jnp.split(inputs, lax.axis_size("dp"), axis=2)), "dp", 0, 0),
+        axis=0,
+    )
 
     def query_side(projected_rows, gain_vector):
         return rotated_unit(projected_rows, gain_vector, token_pos, query_heads)

time: 322 us -> 325 us (level)
  waiting for transfers between devices: 43.6 us -> 93.1 us
  other arithmetic: 49.7 us -> 19.2 us
  local copies, waits for them, and re-layouts: 30 us -> 16.4 us
    all_gather x1, waiting for transfers between devices: 29.1 us -> 79.6 us  [shards(): gathered = lax.all_gather(d_proj, 'dp', axis=0, tiled=True)]
    unnamed x2 -> x1, other arithmetic: 30.4 us -> 0.09 us
    unnamed x27 -> x43, local copies, waits for them, and re-layouts: 21.7 us -> 7.54 us
  transfers between devices with their start and end apart: 15 -> 15, of which waited for: 6 -> 5; matrix products, arithmetic and copies ran while one was open for 24% -> 10% of each run, Pallas kernels for 0% -> 0%
where the time goes in v1:
time: 325 us; the launch traced here: 324 us
  blocking collectives  122 us (38%)
  waiting for transfers between devices  93.1 us (29%)
  matrix products  32.1 us (10%)
  starting transfers between devices  26.3 us (8%)
  other arithmetic  19.2 us (6%)
  local copies, waits for them, and re-layouts  16.4 us (5%)
  between operations  15.3 us (5%)
    all_gather x1, waiting for transfers between devices, shards(): gathered = lax.all_gather(d_proj, 'dp', axis=0, tiled=True)  79.6 us
    all_to_all x1, blocking collectives, shards(): lax.all_to_all(jnp.stack(jnp.split(inputs, lax.axis_size('dp'), axis=2)),...  69.5 us
    psum x1, blocking collectives, shards(): dq_gain_all, dk_gain_all = lax.psum((dq_gain, dk_gain), ('dp', 'ctx'))  52.6 us
    ppermute x12, starting transfers between devices, from_behind(): lax.ppermute(value, axis, [(source, source + steps) for source in range(i...  22.4 us
    ppermute x12, waiting for transfers between devices, from_behind(): lax.ppermute(value, axis, [(source, source + steps) for source in range(i...  13.4 us
    dot_general x1, matrix products, shards(): jnp.einsum('btp,dp->btd', gathered, weight, preferred_element_type=jnp.fl...  10.9 us
    dot_general x1, matrix products, shards(): jnp.einsum('btp,btd->pd', gathered, input_cols, preferred_element_type=jn...  9.82 us
    unnamed x43, local copies, waits for them, and re-layouts  7.54 us
  transfers between devices with their start and end apart: 15, of which 5 were waited for; matrix products, arithmetic and copies ran while one was open for 10% of the time, Pallas kernels for 0%

profile of v1, /device:TPU:0, one launch (start us, length us, event | category | flops | bytes accessed | tf_op | source)
XLA Modules:
  0.0 324.4 jit_solution(14689094630579197068)
XLA Ops:
  7.2 1.1 copy.171
  9.6 0.9 multiply_multiply_fusion.1
  11.0 5.0 %collective-permute-start.2 = (bf16[128,8,128]{2,0,1:T(8,128)(2,1)S(1)}, bf16[128,8,128]{2,0,1:T(8,128)(2,1)}, u32[]{:S(2)}, u32[]{:S(2)}) collective-permute-start(bf16[128,8,128]{2,0,1:T(8,128)(2,1)S(1)} %pad_maximum_fusion.3), channel_id=1, source_target_pairs={{0,3},{4,7},{8,11},{12,15},{16,19},{20,23},{24,27},{28,31}} | collective-permute-start | bytes 786440 | tf_op jit(solution)/shard_map/ppermute | solution.py:16
  16.0 2.0 collective-permute-start
  18.0 2.0 collective-permute-start.1
  20.2 0.9 copy.182
  21.0 2.0 collective-permute-start.3
  23.0 2.0 collective-permute-start.4
  26.8 0.8 maximum_bitcast_fusion.2
  28.6 1.4 reshape_squeeze.7
  30.0 1.2 copy.226
  31.5 1.5 collective-permute-start.5
  33.0 2.1 fusion.7
  35.2 0.9 fusion.6
  36.1 2.8 collective-permute-done.5
  38.9 2.4 fusion.2
  41.4 1.3 fusion.4
  42.7 1.7 fusion.22
  44.4 2.2 fusion.59
  46.6 3.0 fusion.58
  49.6 1.4 copy.238
  51.0 1.4 copy.239
  52.4 0.9 slice_bitcast_fusion.7
  53.3 1.3 collective-permute-start.6
  54.6 1.3 collective-permute-start.7
  55.9 1.3 collective-permute-start.8
  57.2 1.5 multiply_add_fusion.1
  58.8 0.9 multiply_reduce_fusion
  59.9 1.8 fusion.23
  61.6 1.3 concatenate.51
  62.9 1.2 slice_bitcast_fusion.4
  64.1 1.4 collective-permute-start.10
  65.5 1.3 collective-permute-start.11
  66.8 1.3 collective-permute-start.9
  68.2 0.9 collective-permute-done.8
  69.1 1.4 fusion.41
  72.1 3.2 collective-permute-done.10
  75.3 6.4 %collective-permute-done.11 = bf16[128,8,128]{0,2,1:T(8,128)(2,1)S(1)} collective-permute-done((bf16[128,8,128]{0,2,1:T(8,128)(2,1)S(1)}, bf16[128,8,128]{0,2,1:T(8,128)(2,1)S(1)}, u32[]{:S(2)}, u32[]{:S(2)}) %collective-permute-start.11) | collective-permute-done | bytes 262176 | tf_op jit(solution)/shard_map/ppermute | solution.py:16
  81.7 1.2 fusion.38
  83.0 1.0 pad_maximum_fusion.1
  86.7 69.5 %all_to_all.23 = bf16[8,1,128,672]{2,3,1,0:T(8,128)(2,1)S(1)} all-to-all(bf16[8,1,128,672]{2,3,1,0:T(8,128)(2,1)S(1)} %bitcast_dynamic-update-slice_fusion), channel_id=1, replica_groups=mesh['dp'=8,'ctx'=4] {'dp'}, dimensions={0} | all-to-all | bytes 2752512 | tf_op jit(solution)/shard_map/all_to_all | solution.py:51
  156.2 79.6 %all-gather.2.cloned.1.call-done = bf16[8,128,4096]{2,1,0:T(8,128)(2,1)} async-done(((bf16[1,128,4096]{2,1,0:T(8,128)(2,1)}), bf16[8,128,4096]{2,1,0:T(8,128)(2,1)}) %all-gather.2.cloned.1.call-update) | async-done | bytes 8388624 | tf_op jit(solution)/shard_map/all_gather | solution.py:123
  235.9 9.8 %bitcast_convert_fusion = bf16[4096,672]{0,1:T(8,128)(2,1)} fusion(bf16[8,128,4096]{2,1,0:T(8,128)(2,1)} %all-gather.2.cloned.1.call-done, bf16[8,1,128,672]{2,3,1,0:T(8,128)(2,1)S(1)} %all_to_all.23), kind=kOutput, calls=%fused_computation | convolution fusion | flops 5639897088 | bytes 15269888 | tf_op jit(solution)/shard_map/btp,btd->pd/dot_general | solution.py:129
  245.7 10.9 %fusion.18 = bf16[8,128,672]{1,2,0:T(8,128)(2,1)} fusion(bf16[8,128,4096]{2,1,0:T(8,128)(2,1)} %all-gather.2.cloned.1.call-done, bf16[672,4096]{1,0:T(8,128)(2,1)} %param.19), kind=kOutput, calls=%fused_computation.20 | convolution fusion | flops 5637832704 | bytes 15269888 | tf_op jit(solution)/shard_map/btp,dp->btd/dot_general | solution.py:124
  256.6 3.6 %all-to-all-start = ((bf16[8,128,672]{1,2,0:T(8,128)(2,1)}), bf16[8,128,672]{1,2,0:T(8,128)(2,1)S(1)}, u32[]{:S(2)}, u32[]{:S(2)}) async-start(bf16[8,128,672]{1,2,0:T(8,128)(2,1)} %fusion.18), calls=%async_computation | async-start | bytes 2752512 | tf_op jit(solution)/shard_map/all_to_all | solution.py:125
  260.2 52.6 %all-reduce.4 = (f32[128]{0:T(128)}, f32[128]{0:T(128)}) all-reduce(f32[128]{0:T(128)S(1)} %get-tuple-element.24, f32[128]{0:T(128)S(1)} %get-tuple-element.26), channel_id=1, replica_groups=mesh['dp'=8,'ctx'=4] {'dp','ctx'}, use_global_device_ids=true, to_apply=%region_9.10 | all-reduce | flops 256 | bytes 2048 | tf_op jit(solution)/shard_map/psum | solution.py:120
  312.9 1.5 copy.214
  314.4 3.2 convert_element_type.126
  (87 shorter events, 8.7 us)
Async XLA Ops:
  7.2 228.7 %all-gather.2.cloned.1.call-start = ((), (), s32[]{:S(2)}) async-start(), calls=%async_computation.3 | async-start | bytes 9437184 | tf_op jit(solution)/shard_map/all_gather | solution.py:123
  8.4 11.6 %copy-start.7 = (bf16[1,128,1024]{2,1,0:T(8,128)(2,1)S(1)}, bf16[1,128,1024]{2,1,0:T(8,128)(2,1)}, u32[]{:S(2)}) copy-start(bf16[1,128,1024]{2,1,0:T(8,128)(2,1)} %param.13) | copy-start | bytes 786436
  8.6 11.6 %copy-start = (f32[128,8,128]{2,0,1:T(8,128)}, f32[128,8,128]{2,0,1:T(8,128)S(1)}, u32[]{:S(2)}) copy-start(f32[128,8,128]{2,0,1:T(8,128)S(1)} %copy.172) | copy-start | bytes 1572868
  9.6 15.4 %copy-start.4 = (bf16[1,128,2048]{2,1,0:T(8,128)(2,1)S(1)}, bf16[1,128,2048]{2,1,0:T(8,128)(2,1)}, u32[]{:S(2)}) copy-start(bf16[1,128,2048]{2,1,0:T(8,128)(2,1)} %param.11) | copy-start | bytes 1572868
  11.0 20.6 %collective-permute-start.2 = (bf16[128,8,128]{2,0,1:T(8,128)(2,1)S(1)}, bf16[128,8,128]{2,0,1:T(8,128)(2,1)}, u32[]{:S(2)}, u32[]{:S(2)}) collective-permute-start(bf16[128,8,128]{2,0,1:T(8,128)(2,1)S(1)} %pad_maximum_fusion.3), channel_id=1, source_target_pairs={{0,3},{4,7},{8,11},{12,15},{16,19},{20,23},{24,27},{28,31}} | collective-permute-start | bytes 786440 | tf_op jit(solution)/shard_map/ppermute | solution.py:16
  16.0 17.0 %collective-permute-start = (bf16[128,8,128]{2,0,1:T(8,128)(2,1)S(1)}, bf16[128,8,128]{2,0,1:T(8,128)(2,1)}, u32[]{:S(2)}, u32[]{:S(2)}) collective-permute-start(bf16[128,8,128]{2,0,1:T(8,128)(2,1)S(1)} %pad_maximum_fusion.3), channel_id=1, source_target_pairs={{0,1},{1,2},{2,3},{4,5},{5,6},{6,7},{8,9},{9,10},{10,11},{12,13},{... | collective-permute-start | bytes 786440 | tf_op jit(solution)/shard_map/ppermute | solution.py:16
  18.0 15.0 %collective-permute-start.1 = (bf16[128,8,128]{2,0,1:T(8,128)(2,1)S(1)}, bf16[128,8,128]{2,0,1:T(8,128)(2,1)}, u32[]{:S(2)}, u32[]{:S(2)}) collective-permute-start(bf16[128,8,128]{2,0,1:T(8,128)(2,1)S(1)} %pad_maximum_fusion.3), channel_id=1, source_target_pairs={{0,2},{1,3},{4,6},{5,7},{8,10},{9,11},{12,14},{13,15},{16,18},{17,... | collective-permute-start | bytes 786440 | tf_op jit(solution)/shard_map/ppermute | solution.py:16
  21.0 15.0 %collective-permute-start.3 = (bf16[128,8,128]{2,0,1:T(8,128)(2,1)}, bf16[128,8,128]{2,0,1:T(8,128)(2,1)}, u32[]{:S(2)}, u32[]{:S(2)}) collective-permute-start(bf16[128,8,128]{2,0,1:T(8,128)(2,1)} %copy.182), channel_id=1, source_target_pairs={{0,1},{1,2},{2,3},{4,5},{5,6},{6,7},{8,9},{9,10},{10,11},{12,13},{... | collective-permute-start | bytes 786440 | tf_op jit(solution)/shard_map/ppermute | solution.py:16
  23.0 13.1 %collective-permute-start.4 = (bf16[128,8,128]{2,0,1:T(8,128)(2,1)}, bf16[128,8,128]{2,0,1:T(8,128)(2,1)}, u32[]{:S(2)}, u32[]{:S(2)}) collective-permute-start(bf16[128,8,128]{2,0,1:T(8,128)(2,1)} %copy.182), channel_id=1, source_target_pairs={{0,2},{1,3},{4,6},{5,7},{8,10},{9,11},{12,14},{13,15},{16,18},{17,... | collective-permute-start | bytes 786440 | tf_op jit(solution)/shard_map/ppermute | solution.py:16
  25.0 0.8 copy-start.8
  27.8 3.6 %copy-start.10 = (s32[1,128]{1,0:T(1,128)S(1)}, s32[1,128]{1,0:T(1,128)}, u32[]{:S(2)}) copy-start(s32[1,128]{1,0:T(1,128)} %param.15) | copy-start | bytes 1540
  31.5 7.4 %collective-permute-start.5 = (bf16[128,8,128]{2,0,1:T(8,128)(2,1)}, bf16[128,8,128]{2,0,1:T(8,128)(2,1)S(1)}, u32[]{:S(2)}, u32[]{:S(2)}) collective-permute-start(bf16[128,8,128]{2,0,1:T(8,128)(2,1)} %copy.182), channel_id=1, source_target_pairs={{0,3},{4,7},{8,11},{12,15},{16,19},{20,23},{24,27},{28,31}} | collective-permute-start | bytes 786440 | tf_op jit(solution)/shard_map/ppermute | solution.py:16
  35.2 3.7 %copy-start.5 = (bf16[128,8,2,128,1]{0,3,2,4,1:T(8,128)(2,1)S(1)}, bf16[128,8,2,128,1]{0,3,2,4,1:T(8,128)(2,1)}, u32[]{:S(2)}) copy-start(bf16[128,8,2,128,1]{0,3,2,4,1:T(8,128)(2,1)} %copy.226) | copy-start | bytes 1572868
  41.4 1.4 copy-start.6
  52.4 4.8 %copy-start.2 = (f32[128,16,64]{2,1,0:T(8,128)S(1)}, f32[128,16,64]{2,1,0:T(8,128)}, u32[]{:S(2)}) copy-start(f32[128,16,64]{2,1,0:T(8,128)} %copy.238) | copy-start | bytes 1572868
  53.3 13.5 %collective-permute-start.6 = (bf16[128,8,128]{2,0,1:T(8,128)(2,1)}, bf16[128,8,128]{2,0,1:T(8,128)(2,1)}, u32[]{:S(2)}, u32[]{:S(2)}) collective-permute-start(bf16[128,8,128]{2,0,1:T(8,128)(2,1)} %get-tuple-element.44), channel_id=1, source_target_pairs={{1,0},{2,1},{3,2},{5,4},{6,5},{7,6},{9,8},{10,9},{11,10},{13,12},{... | collective-permute-start | bytes 786440 | tf_op jit(solution)/shard_map/ppermute | solution.py:16
  54.6 13.5 %collective-permute-start.7 = (bf16[128,8,128]{2,0,1:T(8,128)(2,1)}, bf16[128,8,128]{2,0,1:T(8,128)(2,1)}, u32[]{:S(2)}, u32[]{:S(2)}) collective-permute-start(bf16[128,8,128]{2,0,1:T(8,128)(2,1)} %get-tuple-element.46), channel_id=1, source_target_pairs={{2,0},{3,1},{6,4},{7,5},{10,8},{11,9},{14,12},{15,13},{18,16},{19,... | collective-permute-start | bytes 786440 | tf_op jit(solution)/shard_map/ppermute | solution.py:16
  55.9 13.2 %collective-permute-start.8 = (bf16[128,8,128]{2,0,1:T(8,128)(2,1)}, bf16[128,8,128]{2,0,1:T(8,128)(2,1)}, u32[]{:S(2)}, u32[]{:S(2)}) collective-permute-start(bf16[128,8,128]{2,0,1:T(8,128)(2,1)} %get-tuple-element.45), channel_id=1, source_target_pairs={{3,0},{7,4},{11,8},{15,12},{19,16},{23,20},{27,24},{31,28}} | collective-permute-start | bytes 786440 | tf_op jit(solution)/shard_map/ppermute | solution.py:16
  64.1 6.7 %copy-start.1 = (f32[128,8,128]{2,0,1:T(8,128)S(1)}, f32[128,8,128]{2,0,1:T(8,128)}, u32[]{:S(2)}) copy-start(f32[128,8,128]{2,0,1:T(8,128)} %copy-done) | copy-start | bytes 1572868
  64.1 6.7 %copy-start.9 = (f32[128]{0:T(128)S(1)}, f32[128]{0:T(128)}, u32[]{:S(2)}) copy-start(f32[128]{0:T(128)} %param.18) | copy-start | bytes 1540
  64.1 11.2 %collective-permute-start.10 = (bf16[128,8,128]{0,2,1:T(8,128)(2,1)S(1)}, bf16[128,8,128]{0,2,1:T(8,128)(2,1)S(1)}, u32[]{:S(2)}, u32[]{:S(2)}) collective-permute-start(bf16[128,8,128]{0,2,1:T(8,128)(2,1)S(1)} %get-tuple-element.49), channel_id=1, source_target_pairs={{2,0},{3,1},{6,4},{7,5},{10,8},{11,9},{14,12},{15,13},{18,16},{19,... | collective-permute-start | bytes 786440 | tf_op jit(solution)/shard_map/ppermute | solution.py:16
  65.5 16.2 %collective-permute-start.11 = (bf16[128,8,128]{0,2,1:T(8,128)(2,1)S(1)}, bf16[128,8,128]{0,2,1:T(8,128)(2,1)S(1)}, u32[]{:S(2)}, u32[]{:S(2)}) collective-permute-start(bf16[128,8,128]{0,2,1:T(8,128)(2,1)S(1)} %get-tuple-element.48), channel_id=1, source_target_pairs={{3,0},{7,4},{11,8},{15,12},{19,16},{23,20},{27,24},{31,28}} | collective-permute-start | bytes 786440 | tf_op jit(solution)/shard_map/ppermute | solution.py:16
  66.8 14.9 %collective-permute-start.9 = (bf16[128,8,128]{0,2,1:T(8,128)(2,1)S(1)}, bf16[128,8,128]{0,2,1:T(8,128)(2,1)S(1)}, u32[]{:S(2)}, u32[]{:S(2)}) collective-permute-start(bf16[128,8,128]{0,2,1:T(8,128)(2,1)S(1)} %get-tuple-element.47), channel_id=1, source_target_pairs={{1,0},{2,1},{3,2},{5,4},{6,5},{7,6},{9,8},{10,9},{11,10},{13,12},{... | collective-permute-start | bytes 786440 | tf_op jit(solution)/shard_map/ppermute | solution.py:16
  82.9 1.7 copy-start.3
  84.1 230.3 %reduce-scatter.2.cloned.1.call-start = ((), (), s32[]{:S(2)}) async-start(), calls=%async_computation.4 | async-start | bytes 6881280 | tf_op jit(solution)/shard_map/reduce_scatter | solution.py:128
  256.6 56.2 %all-to-all-start = ((bf16[8,128,672]{1,2,0:T(8,128)(2,1)}), bf16[8,128,672]{1,2,0:T(8,128)(2,1)S(1)}, u32[]{:S(2)}, u32[]{:S(2)}) async-start(bf16[8,128,672]{1,2,0:T(8,128)(2,1)} %fusion.18), calls=%async_computation | async-start | bytes 2752512 | tf_op jit(solution)/shard_map/all_to_all | solution.py:125
Sparse Core Ops, SparseCore 0:
  84.2 151.5 all-gather.1
  245.8 51.9 reduce-scatter.1
